TPU v7x, 256 devices: a whole 4x4x8 slice. The times are simulated.
256 devices in a mesh: list: 32 (over x, y, core), rep: 8 (over z).
Axes of the slice: x: 4, y: 4, z: 8, core: 2. Of those that a mesh axis runs over, the one named last changes fastest.
Arguments:
- memory_rows: bfloat16 [65536, 1024], P(('list', 'rep'))
- list_owner: int32 [65536, 1], P(('list', 'rep')), may hold values from 0 to 31; in each aligned block of 256 rows (0 to 255, 256 to 511, ...) at most 32 rows name the same one
- list_slot: int32 [65536], P(('list', 'rep')), may hold values from 0 to 2047
- pq_codes: int32 [65536, 16], P(('list', 'rep')), may hold values from 0 to 255
- valid_rows: int32 [256], P(('list', 'rep')), may hold values from 128 to 256
- centroids: bfloat16 [65536, 1024], P('list'), may hold values from -3 to 3
- codebook: float32 [16, 256, 64], replicated
Outputs:
- new_codebook: float32 [16, 256, 64], P('rep')
- row_error: float32 [65536], P(('list', 'rep'))
Inputs may be any that keep to these rules, and one draw needn't show every extreme that they name: `list_owner`: the rows of one device name one index of list at most 32 times, and some device's rows name one exactly 32 times.
All inputs are finite; a program needn't handle non-finite values.
Results may differ from a plain program's by a relative error of at most 0.0038.
Values may be sent and summed in bfloat16 or wider, within the bound.
A program may use at most 128 MiB of HBM per device.

v0:
```python
import jax
import jax.numpy as jnp
from jax import lax
from jax.sharding import PartitionSpec as P

prior_weight = 4.0


def code_statistics(residual, pq_codes, is_live, codebook):
    row_count = residual.shape[0]
    subspaces = codebook.shape[0]
    code_count = codebook.shape[1]
    width_sub = codebook.shape[2]
    residual = jnp.where(is_live[:, None], residual, 0.0)
    recon = codebook[jnp.arange(subspaces)[None, :], pq_codes].reshape(
        row_count, subspaces * width_sub
    )
    row_error = jnp.where(is_live, jnp.mean((residual - recon) ** 2, axis=1), 0.0)
    rounded = (
        residual.astype(jnp.bfloat16).reshape(row_count, subspaces, width_sub).transpose(1, 0, 2)
    )
    codes_major = pq_codes.T

    def per_subspace(item):
        code_col, part_rows = item
        onehot = ((code_col[:, None] == jnp.arange(code_count)[None, :]) & is_live[:, None]).astype(
            jnp.bfloat16
        )
        sums_one = lax.dot_general(
            onehot, part_rows, (((0,), (0,)), ((), ())), preferred_element_type=jnp.float32
        )
        counts_one = jnp.sum(onehot.astype(jnp.float32), axis=0)
        return (sums_one, counts_one)

    sums, counts = lax.map(per_subspace, (codes_major, rounded))
    return (row_error, sums, counts)


def body(memory_rows, list_owner, list_slot, pq_codes, valid_rows, centroids, codebook):
    row_count = memory_rows.shape[0]
    width = memory_rows.shape[1]
    list_count = centroids.shape[0]
    owners = lax.axis_size("list")
    capacity = 4 * row_count // owners
    is_valid = jnp.arange(row_count) < valid_rows[0]
    target = list_owner[:, 0]
    onehot_dest = ((target[:, None] == jnp.arange(owners)[None, :]) & is_valid[:, None]).astype(
        jnp.int32
    )
    before = jnp.cumsum(onehot_dest, axis=0) - onehot_dest
    slot_rank = jnp.sum(before * onehot_dest, axis=1)
    position = jnp.where(is_valid, target * capacity + slot_rank, owners * capacity)
    taken = jnp.clip(position, 0, owners * capacity - 1)
    total_slots = owners * capacity
    send_rows = (
        jnp.zeros((total_slots, width), jnp.bfloat16).at[position].set(memory_rows, mode="drop")
    )
    send_slot = jnp.full((total_slots,), -1, jnp.int32).at[position].set(list_slot, mode="drop")
    send_codes = (
        jnp.zeros((total_slots, pq_codes.shape[1]), jnp.int32)
        .at[position]
        .set(pq_codes, mode="drop")
    )
    got_rows, got_slot, got_codes = (
        lax.all_to_all(
            send_rows.reshape(owners, capacity, width),
            "list",
            split_axis=0,
            concat_axis=0,
            tiled=True,
        ),
        lax.all_to_all(
            send_slot.reshape(owners, capacity), "list", split_axis=0, concat_axis=0, tiled=True
        ),
        lax.all_to_all(
            send_codes.reshape(owners, capacity, pq_codes.shape[1]),
            "list",
            split_axis=0,
            concat_axis=0,
            tiled=True,
        ),
    )
    got_rows = got_rows.reshape(total_slots, width)
    got_slot = got_slot.reshape(total_slots)
    got_codes = got_codes.reshape(total_slots, pq_codes.shape[1])
    is_live = got_slot >= 0
    centre = centroids[jnp.clip(got_slot, 0, list_count - 1)].astype(jnp.float32)
    residual = got_rows.astype(jnp.float32) - centre
    slot_error, sums, counts = code_statistics(residual, got_codes, is_live, codebook)
    returned = lax.all_to_all(
        slot_error.reshape(owners, capacity), "list", split_axis=0, concat_axis=0, tiled=True
    )
    row_error = jnp.where(is_valid, returned.reshape(total_slots)[taken], 0.0)
    subspaces = codebook.shape[0]
    replicas = lax.axis_size("rep")
    share = subspaces // replicas
    first_sub = lax.axis_index("rep") * share
    sums_all, counts_all = lax.psum((sums, counts), ("list", "rep"))
    sums_mine = lax.dynamic_slice_in_dim(sums_all, first_sub, share, 0)
    counts_mine = lax.dynamic_slice_in_dim(counts_all, first_sub, share, 0)
    old_mine = lax.dynamic_slice_in_dim(codebook, first_sub, share, 0)
    new_codebook = (sums_mine + prior_weight * old_mine) / (counts_mine[:, :, None] + prior_weight)
    return (new_codebook, row_error)


def solution(mesh):
    in_specs = (
        P(("list", "rep"), None),
        P(("list", "rep"), None),
        P(("list", "rep")),
        P(("list", "rep"), None),
        P(("list", "rep")),
        P("list", None),
        P(),
    )
    out_specs = (P("rep", None, None), P(("list", "rep")))
    return jax.shard_map(body, mesh=mesh, in_specs=in_specs, out_specs=out_specs, check_vma=False)
```

profile of v0, /device:TPU:2, one launch (start us, length us, event | category | flops | bytes accessed | tf_op | source)
XLA Modules:
  0.0 582.1 jit_solution(2420515403371690203)
XLA Ops:
  7.8 0.7 fusion.22
  9.3 0.9 fusion.19
  10.2 0.7 compare_select_fusion.2
  10.9 1.6 scatter_custom_fusion.1
  12.5 0.7 all_to_all.17
  13.1 7.6 %all-to-all-start.1 = ((s32[32,1,32]{2,1,0:T(1,128)}), s32[32,1,32]{2,1,0:T(1,128)S(1)}, u32[]{:S(2)}, u32[]{:S(2)}) async-start(s32[32,1,32]{2,1,0:T(1,128)} %all_to_all.17), calls=%async_computation.1 | async-start | bytes 32768 | tf_op jit(solution)/shard_map/all_to_all | solution.py:72
  20.8 0.8 copy.39
  21.6 1.3 scatter_custom_fusion
  23.1 0.8 reshape.243
  23.9 3.1 all-to-all-done.1
  26.9 5.0 all-to-all-start
  31.9 3.7 scatter_custom_fusion.2
  35.6 2.7 all-to-all-done
  38.3 5.8 %all-to-all-start.2 = ((bf16[32,32,1024]{2,1,0:T(8,128)(2,1)}), bf16[32,32,1024]{2,1,0:T(8,128)(2,1)}, u32[]{:S(2)}, u32[]{:S(2)}) async-start(bf16[32,32,1024]{2,1,0:T(8,128)(2,1)} %bitcast.13), calls=%async_computation.2 | async-start | bytes 4194304 | tf_op jit(solution)/shard_map/all_to_all | solution.py:65
  45.2 8.8 %gather_fusion = bf16[1024,1024]{1,0:T(8,128)(2,1)} fusion(bf16[2048,1024]{1,0:T(8,128)(2,1)} %param.14, s32[1024]{0:T(1024)S(1)} %broadcast_clamp_fusion.1), kind=kCustom, calls=%fused_computation | custom fusion | bytes 4198400 | tf_op jit(solution)/shard_map/gather | solution.py:87
  53.9 4.1 copy.44
  58.0 4.0 convert_element_type.53
  62.0 8.1 %copy.45 = f32[1024,16,64]{2,1,0:T(8,128)} copy(f32[1024,16,64]{0,2,1:T(8,128)} %bitcast.73) | data formatting | bytes 8388608 | tf_op jit(solution)/shard_map/convert_element_type | solution.py:87
  70.7 0.8 reduce.8
  72.4 176.0 %gather_fusion.1 = f32[16384,64]{1,0:T(8,128)} fusion(f32[16,256,64]{2,1,0:T(8,128)S(1)} %copy.49, s32[16384]{0:T(1024)S(1)} %reshape.188), kind=kCustom, calls=%fused_computation.1 | custom fusion | bytes 8519680 | tf_op jit(solution)/shard_map/gather | solution.py:15
  248.5 7.6 %gather.13 = f32[32,32,1024]{2,1,0:T(8,128)} reshape(f32[16384,64]{1,0:T(8,128)} %gather_fusion.1) | data formatting | bytes 8388608 | tf_op jit(solution)/shard_map/gather | solution.py:15
  256.1 6.9 %reshape.177 = f32[1024,16,64]{2,1,0:T(8,128)} reshape(bf16[32,32,1024]{2,1,0:T(8,128)(2,1)} %all-to-all-done.2) | data formatting | bytes 6291456 | tf_op jit(solution)/shard_map/convert_element_type | solution.py:88
  262.9 7.7 %fusion.9 = bf16[16,1024,64]{2,0,1:T(8,128)(2,1)S(1)} fusion(f32[1024,16,64]{2,1,0:T(8,128)} %reshape.177, f32[1024,16,64]{2,1,0:T(8,128)} %copy.45, pred[1024]{0:T(1024)(128)(4,1)S(1)} %ge.17), kind=kLoop, calls=%fused_computation.19 | loop fusion | flops 3145728 | bytes 10486784 | tf_op jit(solution)/shard_map/transpose | solution.py:20
  270.6 3.0 copy.46
  273.6 40.9 %while.12 = (s32[]{:T(128)}, f32[16,256,64]{1,2,0:T(8,128)}, f32[16,256]{1,0:T(8,128)S(1)}, s32[16,1024]{1,0:T(8,128)S(1)}, pred[1024]{0:T(1024)(128)(4,1)S(1)},...) while((s32[]{:T(128)}, f32[16,256,64]{1,2,0:T(8,128)}, f32[16,256]{1,0:T(8,128)S(1)}, ...), condition=%wide.region_8.9_spmd, body=%wide.region_6.8_spmd.sunk | while | flops 35389184 | bytes 350301 | solution.py:35
  273.6 2.1 fusion.31
  276.2 2.1 fusion.31
  278.8 2.1 fusion.31
  281.3 2.1 fusion.31
  283.9 2.1 fusion.31
  286.4 2.1 fusion.31
  289.0 2.1 fusion.31
  291.5 2.1 fusion.31
  294.1 2.1 fusion.31
  296.6 2.1 fusion.31
  299.2 2.1 fusion.31
  301.8 2.1 fusion.31
  304.3 2.1 fusion.31
  306.9 2.1 fusion.31
  309.4 2.1 fusion.31
  312.0 2.1 fusion.31
  314.6 5.1 multiply_reduce_fusion
  320.3 7.4 %all-to-all-start.3 = ((f32[32,1,32]{2,1,0:T(1,128)}), f32[32,1,32]{2,1,0:T(1,128)S(1)}, u32[]{:S(2)}, u32[]{:S(2)}) async-start(f32[32,1,32]{2,1,0:T(1,128)} %bitcast.21), calls=%async_computation.3 | async-start | bytes 32768 | tf_op jit(solution)/shard_map/all_to_all | solution.py:90
  327.7 79.8 %psum.15 = f32[16,256]{1,0:T(8,128)S(1)} all-reduce(f32[16,256]{1,0:T(8,128)S(1)} %get-tuple-element.36), channel_id=1, replica_groups=mesh['list'=32,'rep'=8] {'list','rep'}, use_global_device_ids=true, to_apply=%region_10.11 | all-reduce | flops 4096 | bytes 32768 | tf_op jit(solution)/shard_map/psum | solution.py:98
  408.0 0.7 reduce.7
  408.8 1.4 gather_fusion.2
  410.7 162.9 %all-reduce.2.cloned.1.call-done = f32[16,256,64]{1,2,0:T(8,128)} async-done(((f32[16,256,64]{1,2,0:T(8,128)}), f32[16,256,64]{1,2,0:T(8,128)}) %all-reduce.2.cloned.1.call-update) | async-done | bytes 1048592 | tf_op jit(solution)/shard_map/psum | solution.py:98
  573.6 1.6 add_divide_fusion
  (86 shorter events, 11.6 us)
Async XLA Ops:
  9.1 35.3 %copy-start = (f32[16,256,64]{1,2,0:T(8,128)S(1)}, f32[16,256,64]{1,2,0:T(8,128)}, u32[]{:S(2)}) copy-start(f32[16,256,64]{1,2,0:T(8,128)} %param.15) | copy-start | bytes 3145732
  13.1 13.8 %all-to-all-start.1 = ((s32[32,1,32]{2,1,0:T(1,128)}), s32[32,1,32]{2,1,0:T(1,128)S(1)}, u32[]{:S(2)}, u32[]{:S(2)}) async-start(s32[32,1,32]{2,1,0:T(1,128)} %all_to_all.17), calls=%async_computation.1 | async-start | bytes 32768 | tf_op jit(solution)/shard_map/all_to_all | solution.py:72
  26.9 11.4 %all-to-all-start = ((s32[32,1,512]{2,1,0:T(1,128)}), s32[32,1,512]{2,1,0:T(1,128)S(1)}, u32[]{:S(2)}, u32[]{:S(2)}) async-start(s32[32,1,512]{2,1,0:T(1,128)} %reshape.243), calls=%async_computation | async-start | bytes 131072 | tf_op jit(solution)/shard_map/all_to_all | solution.py:75
  38.3 217.7 %all-to-all-start.2 = ((bf16[32,32,1024]{2,1,0:T(8,128)(2,1)}), bf16[32,32,1024]{2,1,0:T(8,128)(2,1)}, u32[]{:S(2)}, u32[]{:S(2)}) async-start(bf16[32,32,1024]{2,1,0:T(8,128)(2,1)} %bitcast.13), calls=%async_computation.2 | async-start | bytes 4194304 | tf_op jit(solution)/shard_map/all_to_all | solution.py:65
  44.2 529.5 %all-reduce.2.cloned.1.call-start = ((), (), s32[]{:S(2)}) async-start(), calls=%async_computation.4 | async-start | bytes 2097152 | tf_op jit(solution)/shard_map/psum | solution.py:98
  320.3 87.2 %all-to-all-start.3 = ((f32[32,1,32]{2,1,0:T(1,128)}), f32[32,1,32]{2,1,0:T(1,128)S(1)}, u32[]{:S(2)}, u32[]{:S(2)}) async-start(f32[32,1,32]{2,1,0:T(1,128)} %bitcast.21), calls=%async_computation.3 | async-start | bytes 32768 | tf_op jit(solution)/shard_map/all_to_all | solution.py:90
Sparse Core Ops, SparseCore 0:
  314.7 258.9 all-reduce.1
where the time goes:
time: 584 us; the launch traced here: 582 us
  local copies, waits for them, and re-layouts  229 us (39%)
  waiting for transfers between devices  169 us (29%)
  blocking collectives  79.8 us (14%)
  matrix products  34 us (6%)
  other arithmetic  29.6 us (5%)
  starting transfers between devices  26.1 us (4%)
  between operations  14.9 us (3%)
    gather x2, local copies, waits for them, and re-layouts, code_statistics(): codebook[jnp.arange(subspaces)[None, :], pq_codes]  184 us
    psum x1, waiting for transfers between devices, body(): sums_all, counts_all = lax.psum((sums, counts), ('list', 'rep'))  163 us
    psum x1, blocking collectives, body(): sums_all, counts_all = lax.psum((sums, counts), ('list', 'rep'))  79.8 us
    dot_general x16, matrix products, per_subspace(): lax.dot_general(onehot, part_rows, (((0,), (0,)), ((), ())), preferred_el...  34 us
    convert_element_type x2, local copies, waits for them, and re-layouts, body(): centroids[jnp.clip(got_slot, 0, list_count - 1)].astype(jnp.float32)  12.2 us
  transfers between devices with their start and end apart: 5, of which 3 were waited for; matrix products, arithmetic and copies ran while one was open for 39% of the time, Pallas kernels for 0%

commit v1 on v0

--- a/solution.py
+++ b/solution.py
@@ -95,7 +95,7 @@
     replicas = lax.axis_size("rep")
     share = subspaces // replicas
     first_sub = lax.axis_index("rep") * share
-    sums_all, counts_all = lax.psum((sums, counts), ("list", "rep"))
+    sums_all, counts_all = lax.psum(lax.psum((sums, counts), "rep"), "list")
     sums_mine = lax.dynamic_slice_in_dim(sums_all, first_sub, share, 0)
     counts_mine = lax.dynamic_slice_in_dim(counts_all, first_sub, share, 0)
     old_mine = lax.dynamic_slice_in_dim(codebook, first_sub, share, 0)

time: 584 us -> 498 us (0.85)
  the two profiles are of different devices: /device:TPU:2 before, /device:TPU:0 now
where the time goes in v1:
time: 498 us; the launch traced here: 497 us
  local copies, waits for them, and re-layouts  227 us (46%)
  blocking collectives  157 us (32%)
  matrix products  34.1 us (7%)
  other arithmetic  29.6 us (6%)
  starting transfers between devices  18.3 us (4%)
  waiting for transfers between devices  15.8 us (3%)
  between operations  14.9 us (3%)
    gather x2, local copies, waits for them, and re-layouts, code_statistics(): codebook[jnp.arange(subspaces)[None, :], pq_codes]  184 us
    psum x2, blocking collectives, body(): sums_all, counts_all = lax.psum(lax.psum((sums, counts), 'rep'), 'list')  157 us
    dot_general x16, matrix products, per_subspace(): lax.dot_general(onehot, part_rows, (((0,), (0,)), ((), ())), preferred_el...  34.1 us
    convert_element_type x2, local copies, waits for them, and re-layouts, body(): centroids[jnp.clip(got_slot, 0, list_count - 1)].astype(jnp.float32)  11.3 us
  transfers between devices with their start and end apart: 6, of which 3 were waited for; matrix products, arithmetic and copies ran while one was open for 45% of the time, Pallas kernels for 0%

profile of v1, /device:TPU:0, one launch (start us, length us, event | category | flops | bytes accessed | tf_op | source)
XLA Modules:
  0.0 496.7 jit_solution(12410762649620290862)
XLA Ops:
  7.8 0.7 fusion.22
  9.3 0.8 fusion.19
  10.1 0.7 compare_select_fusion.2
  10.8 1.6 scatter_custom_fusion.1
  13.1 5.6 %all-to-all-start.1 = ((s32[32,1,32]{2,1,0:T(1,128)}), s32[32,1,32]{2,1,0:T(1,128)S(1)}, u32[]{:S(2)}, u32[]{:S(2)}) async-start(s32[32,1,32]{2,1,0:T(1,128)} %all_to_all.17), calls=%async_computation.1 | async-start | bytes 32768 | tf_op jit(solution)/shard_map/all_to_all | solution.py:72
  18.6 0.8 copy.39
  19.5 1.3 scatter_custom_fusion
  20.9 0.8 reshape.243
  21.7 4.3 all-to-all-done.1
  26.0 3.9 all-to-all-start
  29.9 3.8 scatter_custom_fusion.2
  33.7 3.7 all-to-all-done
  37.4 4.8 all-to-all-start.2
  42.5 7.7 %gather_fusion = bf16[1024,1024]{1,0:T(8,128)(2,1)S(1)} fusion(bf16[2048,1024]{1,0:T(8,128)(2,1)} %param.14, s32[1024]{0:T(1024)S(1)} %broadcast_clamp_fusion.1), kind=kCustom, calls=%fused_computation | custom fusion | bytes 4198400 | tf_op jit(solution)/shard_map/gather | solution.py:87
  50.3 3.2 copy.44
  53.4 8.1 %copy.45 = f32[1024,16,64]{2,1,0:T(8,128)} copy(f32[1024,16,64]{0,2,1:T(8,128)} %bitcast.73) | data formatting | bytes 8388608 | tf_op jit(solution)/shard_map/convert_element_type | solution.py:87
  62.1 0.8 reduce.8
  63.3 7.7 %all-to-all-done.2 = bf16[32,32,1024]{2,1,0:T(8,128)(2,1)} async-done(((bf16[32,32,1024]{2,1,0:T(8,128)(2,1)}), bf16[32,32,1024]{2,1,0:T(8,128)(2,1)}, u32[]{:S(2)}, u32[]{:S(2)}) %all-to-all-start.2) | async-done | bytes 2097184 | tf_op jit(solution)/shard_map/all_to_all | solution.py:65
  71.0 6.9 %reshape.177 = f32[1024,16,64]{2,1,0:T(8,128)} reshape(bf16[32,32,1024]{2,1,0:T(8,128)(2,1)} %all-to-all-done.2) | data formatting | bytes 6291456 | tf_op jit(solution)/shard_map/convert_element_type | solution.py:88
  77.9 7.7 %fusion.9 = bf16[16,1024,64]{2,0,1:T(8,128)(2,1)S(1)} fusion(f32[1024,16,64]{2,1,0:T(8,128)} %reshape.177, f32[1024,16,64]{2,1,0:T(8,128)} %copy.45, pred[1024]{0:T(1024)(128)(4,1)S(1)} %ge.17), kind=kLoop, calls=%fused_computation.19 | loop fusion | flops 3145728 | bytes 10486784 | tf_op jit(solution)/shard_map/transpose | solution.py:20
  85.6 3.0 copy.46
  88.6 41.0 %while.12 = (s32[]{:T(128)}, f32[16,256,64]{1,2,0:T(8,128)}, f32[16,256]{1,0:T(8,128)S(1)}, s32[16,1024]{1,0:T(8,128)S(1)}, pred[1024]{0:T(1024)(128)(4,1)S(1)},...) while((s32[]{:T(128)}, f32[16,256,64]{1,2,0:T(8,128)}, f32[16,256]{1,0:T(8,128)S(1)}, ...), condition=%wide.region_8.9_spmd, body=%wide.region_6.8_spmd.sunk | while | flops 35389184 | bytes 350301 | solution.py:35
  88.6 2.2 fusion.31
  91.3 2.1 fusion.31
  93.8 2.1 fusion.31
  96.4 2.1 fusion.31
  98.9 2.1 fusion.31
  101.5 2.1 fusion.31
  104.0 2.1 fusion.31
  106.6 2.1 fusion.31
  109.2 2.1 fusion.31
  111.7 2.1 fusion.31
  114.3 2.1 fusion.31
  116.8 2.1 fusion.31
  119.4 2.1 fusion.31
  121.9 2.1 fusion.31
  124.5 2.1 fusion.31
  127.1 2.1 fusion.31
  130.3 4.0 convert_element_type.53
  134.9 176.0 %gather_fusion.1 = f32[16384,64]{1,0:T(8,128)} fusion(f32[16,256,64]{2,1,0:T(8,128)S(1)} %copy.49, s32[16384]{0:T(1024)S(1)} %reshape.188), kind=kCustom, calls=%fused_computation.1 | custom fusion | bytes 8519680 | tf_op jit(solution)/shard_map/gather | solution.py:15
  310.9 7.6 %gather.13 = f32[32,32,1024]{2,1,0:T(8,128)} reshape(f32[16384,64]{1,0:T(8,128)} %gather_fusion.1) | data formatting | bytes 8388608 | tf_op jit(solution)/shard_map/gather | solution.py:15
  318.6 5.1 %multiply_reduce_fusion = f32[32,32]{1,0:T(8,128)S(1)} fusion(f32[32,32,1024]{2,1,0:T(8,128)} %gather.13, f32[32,32,1024]{2,1,0:T(8,128)} %bitcast.74, pred[32,32]{1,0:T(8,128)(4,1)S(1)} %fusion.25, bf16[32,32,1024]{2,1,0:T(8,128)(2,1)} %all-to-all-done.2), kind=kLoop, calls=%fused_computation.20 | loop fusion | flops 6290432 | bytes 10490880 | tf_op jit(solution)/shard_map/reduce_sum | solution.py:18
  324.3 3.8 all-to-all-start.3
  328.1 32.8 %psum.30 = f32[16,256]{1,0:T(8,128)S(1)} all-reduce(f32[16,256]{1,0:T(8,128)S(1)} %get-tuple-element.36), channel_id=1, replica_groups=mesh['list'=32,'rep'=8] {'rep'}, use_global_device_ids=true, to_apply=%region_11.12 | all-reduce | flops 4096 | bytes 32768 | tf_op jit(solution)/shard_map/psum | solution.py:98
  360.9 124.1 %psum.31 = f32[16,256]{1,0:T(8,128)S(1)} all-reduce(f32[16,256]{1,0:T(8,128)S(1)} %psum.30), channel_id=1, replica_groups=mesh['list'=32,'rep'=8] {'list'}, use_global_device_ids=true, to_apply=%region_12.13 | all-reduce | flops 4096 | bytes 32768 | tf_op jit(solution)/shard_map/psum | solution.py:98
  485.5 0.7 reduce.7
  486.2 1.4 gather_fusion.2
  488.2 1.6 add_divide_fusion
  (92 shorter events, 12.4 us)
Async XLA Ops:
  13.1 13.0 %all-to-all-start.1 = ((s32[32,1,32]{2,1,0:T(1,128)}), s32[32,1,32]{2,1,0:T(1,128)S(1)}, u32[]{:S(2)}, u32[]{:S(2)}) async-start(s32[32,1,32]{2,1,0:T(1,128)} %all_to_all.17), calls=%async_computation.1 | async-start | bytes 32768 | tf_op jit(solution)/shard_map/all_to_all | solution.py:72
  26.0 11.4 %all-to-all-start = ((s32[32,1,512]{2,1,0:T(1,128)}), s32[32,1,512]{2,1,0:T(1,128)S(1)}, u32[]{:S(2)}, u32[]{:S(2)}) async-start(s32[32,1,512]{2,1,0:T(1,128)} %reshape.243), calls=%async_computation | async-start | bytes 131072 | tf_op jit(solution)/shard_map/all_to_all | solution.py:75
  37.4 33.6 %all-to-all-start.2 = ((bf16[32,32,1024]{2,1,0:T(8,128)(2,1)}), bf16[32,32,1024]{2,1,0:T(8,128)(2,1)}, u32[]{:S(2)}, u32[]{:S(2)}) async-start(bf16[32,32,1024]{2,1,0:T(8,128)(2,1)} %bitcast.13), calls=%async_computation.2 | async-start | bytes 4194304 | tf_op jit(solution)/shard_map/all_to_all | solution.py:65
  42.2 281.5 %all-reduce.3.cloned.1.call-start = ((), (), s32[]{:S(2)}) async-start(), calls=%async_computation.4 | async-start | bytes 2097152 | tf_op jit(solution)/shard_map/psum | solution.py:98
  50.2 11.3 %copy-start = (bf16[1024,1024]{1,0:T(8,128)(2,1)}, bf16[1024,1024]{1,0:T(8,128)(2,1)S(1)}, u32[]{:S(2)}) copy-start(bf16[1024,1024]{1,0:T(8,128)(2,1)S(1)} %gather_fusion) | copy-start | bytes 6291460
  88.6 41.1 %copy-start.1 = (f32[16,256,64]{1,2,0:T(8,128)S(1)}, f32[16,256,64]{1,2,0:T(8,128)}, u32[]{:S(2)}) copy-start(f32[16,256,64]{1,2,0:T(8,128)} %param.15) | copy-start | bytes 3145732
  129.6 358.6 %all-reduce.5.cloned.1.call-start = ((), (), s32[]{:S(2)}) async-start(), calls=%async_computation.5 | async-start | bytes 2097152 | tf_op jit(solution)/shard_map/psum | solution.py:98
  324.3 160.7 %all-to-all-start.3 = ((f32[32,1,32]{2,1,0:T(1,128)}), f32[32,1,32]{2,1,0:T(1,128)S(1)}, u32[]{:S(2)}, u32[]{:S(2)}) async-start(f32[32,1,32]{2,1,0:T(1,128)} %bitcast.21), calls=%async_computation.3 | async-start | bytes 32768 | tf_op jit(solution)/shard_map/all_to_all | solution.py:90
Sparse Core Ops, SparseCore 0:
  129.7 75.0 all-reduce.2
  323.8 114.1 all-reduce.4
